TPU v7x, 32 devices: a whole 2x2x4 slice. The times are simulated.
32 devices in a mesh: section: 4 (over x, core), mp: 8 (over z, y).
Axes of the slice: x: 2, y: 2, z: 4, core: 2. Of those that a mesh axis runs over, the one named last changes fastest.
Arguments:
- activations: bfloat16 [4, 64, 4096], P('section', 'mp'), may hold values from -24 to 24
- enc_weight: bfloat16 [4, 4096, 4096], P('section', None, 'mp'), may hold values from -0.046875 to 0.046875
- enc_bias: float32 [4096], P('mp'), may hold values from -4 to 4
- dec_weight: bfloat16 [4096, 4, 4096], P('mp', 'section'), may hold values from -2.1875 to 2.1875
- dec_bias: float32 [4, 4096], P('section'), may hold values from -3 to 3
Outputs:
- loss: float32 [], replicated
- grad_dec: bfloat16 [4096, 4, 4096], P('mp', 'section')
- grad_bias: float32 [4, 4096], P('section', 'mp')
All inputs are finite; a program needn't handle non-finite values.
Results may differ from a plain program's by a relative error of at most 0.009.
Values may be sent and summed in bfloat16 or wider, within the bound.
A program may use at most 64 MiB of HBM per device.

v0:
```python
import jax
import jax.numpy as jnp
from jax import lax
from jax.sharding import PartitionSpec as P

penalty_weight = 2.0


def local(activations, enc_weight, enc_bias, dec_weight, dec_bias):
    all_rows = lax.all_gather(activations[0], "mp", axis=0, tiled=True)
    token_count = all_rows.shape[0]
    partial_value = jnp.dot(all_rows, enc_weight[0], preferred_element_type=jnp.float32)
    w_dec = dec_weight[:, 0, :]
    layer_norm = jnp.sqrt(jnp.sum(jnp.square(w_dec.astype(jnp.float32)), axis=1) + 1e-06)
    pre_sum, norm_total = (
        lax.psum(partial_value.astype(jnp.bfloat16), "section").astype(jnp.float32),
        lax.psum(layer_norm.astype(jnp.bfloat16), "section").astype(jnp.float32),
    )
    latents = jnp.maximum(pre_sum + enc_bias[None, :], 0.0).astype(jnp.bfloat16)
    latent_float = latents.astype(jnp.float32)
    latent_sum = jnp.sum(latent_float, axis=0)
    penalty_part = penalty_weight / token_count * jnp.sum(latent_float * norm_total[None, :])
    penalty_part = jnp.where(lax.axis_index("section") == 0, penalty_part, 0.0)
    coef = penalty_weight * latent_sum / token_count / layer_norm
    col_width = w_dec.shape[1] // lax.axis_size("mp")
    first_col = lax.axis_index("mp") * col_width
    recon_t = lax.psum_scatter(
        lax.dot_general(
            w_dec, latents, (((0,), (1,)), ((), ())), preferred_element_type=jnp.float32
        ),
        "mp",
        scatter_dimension=0,
        tiled=True,
    )
    bias_cols = lax.dynamic_slice_in_dim(dec_bias[0], first_col, col_width, 0)
    x_cols = lax.dynamic_slice_in_dim(all_rows, first_col, col_width, 1)
    error_cols = recon_t + bias_cols[:, None] - x_cols.T.astype(jnp.float32)
    square_sum = jnp.sum(error_cols * error_cols)
    scaled = 2.0 * error_cols / token_count
    grad_rec_t = scaled.astype(jnp.bfloat16)
    grad_bias = jnp.sum(scaled, axis=1)[None, :]
    grad_sum = lax.dot_general(
        latents,
        lax.all_gather(grad_rec_t, "mp", axis=0, tiled=True),
        (((0,), (1,)), ((), ())),
        preferred_element_type=jnp.float32,
    )
    grad_dec = (grad_sum + coef[:, None] * w_dec.astype(jnp.float32)).astype(jnp.bfloat16)[
        :, None, :
    ]
    loss = lax.psum(square_sum / token_count + penalty_part, ("section", "mp"))
    return (loss, grad_dec, grad_bias)


def solution(mesh):
    in_specs = (
        P("section", "mp", None),
        P("section", None, "mp"),
        P("mp"),
        P("mp", "section", None),
        P("section", None),
    )
    out_specs = (P(), P("mp", "section", None), P("section", "mp"))
    return jax.shard_map(local, mesh=mesh, in_specs=in_specs, out_specs=out_specs, check_vma=False)
```

profile of v0, /device:TPU:0, one launch (start us, length us, event | category | flops | bytes accessed | tf_op | source)
XLA Modules:
  0.0 231.0 jit_solution(3103381486748929811)
XLA Ops:
  7.2 0.0 copy-start
  7.2 0.0 copy-start.2
  7.2 0.0 all-reduce.2.cloned.1.call-start
  7.2 33.2 %all-gather = bf16[1,64,4096]{2,1,0:T(8,128)(2,1)S(1)} all-gather(bf16[1,8,4096]{2,1,0:T(8,128)(2,1)} %param.5), channel_id=2, replica_groups=mesh['section'=4,'mp'=8] {'mp'}, dimensions={1}, use_global_device_ids=true | all-gather | bytes 589824 | tf_op jit(solution)/shard_map/all_gather | solution.py:10
  40.5 3.7 %fusion.7 = bf16[64,512]{1,0:T(8,128)(2,1)} fusion(bf16[1,4096,512]{2,1,0:T(8,128)(2,1)} %param.6, bf16[1,64,4096]{2,1,0:T(8,128)(2,1)S(1)} %all-gather), kind=kOutput, calls=%fused_computation.10 | convolution fusion | flops 268468224 | bytes 4784128 | tf_op jit(solution)/shard_map/dot_general | solution.py:12
  44.1 0.0 all-reduce.2.cloned.1.call-update
  44.2 0.0 reduce-scatter.2.cloned.1.call-start
  44.2 32.7 %all-reduce.2.cloned.1.call-done = bf16[64,512]{1,0:T(8,128)(2,1)} async-done(((bf16[64,512]{1,0:T(8,128)(2,1)}), bf16[64,512]{1,0:T(8,128)(2,1)}) %all-reduce.2.cloned.1.call-update) | async-done | bytes 65552 | tf_op jit(solution)/shard_map/psum | solution.py:16
  76.9 0.0 copy-done.2
  76.9 0.0 copy-start.1
  76.9 4.1 %convolution_bitcast_fusion = f32[4096,64]{0,1:T(8,128)} fusion(bf16[512,1,4096]{2,0,1:T(8,128)(2,1)} %param.8, bf16[64,512]{1,0:T(8,128)(2,1)} %all-reduce.2.cloned.1.call-done, f32[512]{0:T(512)S(1)} %copy-done.2), kind=kOutput, calls=%fused_computation.6 | convolution fusion | flops 268566528 | bytes 5310464 | tf_op jit(solution)/shard_map/dot_general | solution.py:28
  81.0 0.0 reduce-scatter.2.cloned.1.call-update
  81.1 3.1 %fusion = f32[512]{0:T(512)S(1)} fusion(bf16[512,1,4096]{2,0,1:T(8,128)(2,1)} %param.8), kind=kLoop, calls=%fused_computation.2 | loop fusion | flops 6290944 | bytes 4196352 | tf_op jit(solution)/shard_map/reduce_sum | solution.py:14
  84.1 5.8 %psum.22 = bf16[512]{0:T(512)(128)(2,1)S(1)} all-reduce(bf16[512]{0:T(512)(128)(2,1)S(1)} %sqrt_convert_fusion), channel_id=1, replica_groups=mesh['section'=4,'mp'=8] {'section'}, use_global_device_ids=true, to_apply=%region_4.0 | all-reduce | flops 512 | bytes 2048 | tf_op jit(solution)/shard_map/psum | solution.py:17
  89.9 0.0 copy-done
  89.9 0.0 copy-done.1
  89.9 0.6 convert_reduce_fusion
  91.2 54.2 %reduce-scatter.2.cloned.1.call-done = f32[512,64]{0,1:T(8,128)} async-done(((f32[4096,64]{0,1:T(8,128)}), f32[512,64]{0,1:T(8,128)}) %reduce-scatter.2.cloned.1.call-update) | async-done | bytes 131088 | tf_op jit(solution)/shard_map/reduce_scatter | solution.py:27
  145.5 1.5 multiply_reduce_fusion.1
  147.7 39.8 %psum.23 = f32[]{:T(128)} all-reduce(f32[]{:T(128)S(6)} %add.54), channel_id=1, replica_groups=mesh['section'=4,'mp'=8] {'section','mp'}, use_global_device_ids=true, to_apply=%region_6.7 | all-reduce | flops 1 | bytes 8 | tf_op jit(solution)/shard_map/psum | solution.py:51
  187.5 31.2 %all_gather.7 = bf16[4096,64]{0,1:T(8,128)(2,1)S(1)} all-gather(bf16[512,64]{0,1:T(8,128)(2,1)S(1)} %get-tuple-element.7), channel_id=1, replica_groups=mesh['section'=4,'mp'=8] {'mp'}, dimensions={0}, use_global_device_ids=true | all-gather | bytes 589824 | tf_op jit(solution)/shard_map/all_gather | solution.py:44
  218.7 5.5 %fusion.3 = bf16[512,1,4096]{2,0,1:T(8,128)(2,1)} fusion(bf16[4096,64]{0,1:T(8,128)(2,1)S(1)} %all_gather.7, bf16[512,1,4096]{2,0,1:T(8,128)(2,1)} %param.8, f32[512]{0:T(512)S(1)} %rsqrt_multiply_fusion, bf16[64,512]{1,0:T(8,128)(2,1)S(1)} %copy-done.1, f32[512]{0:T(512)S(1)} %copy-done.2), kind=kOutput, calls=%fused_computation.5 | convolution fusion | flops 276955136 | bytes 8982528 | tf_op jit(solution)/shard_map/dot_general | solution.py:42
  (4 shorter events, 0.0 us)
Async XLA Ops:
  7.2 82.8 %copy-start = (f32[1,4096]{1,0:T(1,128)S(1)}, f32[1,4096]{1,0:T(1,128)}, u32[]{:S(2)}) copy-start(f32[1,4096]{1,0:T(1,128)} %param.9) | copy-start | bytes 49156
  7.2 69.8 %copy-start.2 = (f32[512]{0:T(512)S(1)}, f32[512]{0:T(512)}, u32[]{:S(2)}) copy-start(f32[512]{0:T(512)} %param.7) | copy-start | bytes 6148
  7.2 69.8 %all-reduce.2.cloned.1.call-start = ((), (), s32[]{:S(2)}) async-start(), calls=%async_computation.1 | async-start | bytes 131072 | tf_op jit(solution)/shard_map/psum | solution.py:16
  44.2 101.3 %reduce-scatter.2.cloned.1.call-start = ((), (), s32[]{:S(2)}) async-start(), calls=%async_computation.2 | async-start | bytes 1179648 | tf_op jit(solution)/shard_map/reduce_scatter | solution.py:27
  76.9 13.0 %copy-start.1 = (bf16[64,512]{1,0:T(8,128)(2,1)S(1)}, bf16[64,512]{1,0:T(8,128)(2,1)}, u32[]{:S(2)}) copy-start(bf16[64,512]{1,0:T(8,128)(2,1)} %all-reduce.2.cloned.1.call-done) | copy-start | bytes 196612
Sparse Core Ops, SparseCore 0:
  44.3 32.6 all-reduce.1
  81.2 64.2 reduce-scatter.1
where the time goes:
time: 231 us
  blocking collectives  110 us (48%)
  waiting for transfers between devices  87 us (38%)
  between operations  15.4 us (7%)
  matrix products  13.2 us (6%)
  other arithmetic  5.29 us (2%)
    reduce_scatter x1, waiting for transfers between devices, local(): lax.psum_scatter(lax.dot_general(w_dec, latents, (((0,), (1,)), ((), ()))...  54.2 us
    psum x1, blocking collectives, local(): loss = lax.psum(square_sum / token_count + penalty_part, ('section', 'mp'))  39.8 us
    all_gather x1, blocking collectives, local(): all_rows = lax.all_gather(activations[0], 'mp', axis=0, tiled=True)  33.2 us
    psum x1, waiting for transfers between devices, local(): lax.psum(partial_value.astype(jnp.bfloat16), 'section').astype(jnp.float32)  32.7 us
    all_gather x1, blocking collectives, local(): lax.all_gather(grad_rec_t, 'mp', axis=0, tiled=True)  31.2 us
    psum x1, blocking collectives, local(): lax.psum(layer_norm.astype(jnp.bfloat16), 'section').astype(jnp.float32)  5.77 us
    dot_general x1, matrix products, local(): lax.dot_general(latents, lax.all_gather(grad_rec_t, 'mp', axis=0, tiled=T...  5.49 us
  transfers between devices with their start and end apart: 2, of which 2 were waited for; matrix products, arithmetic and copies ran while one was open for 2% of the time, Pallas kernels for 0%

commit v1 on v0

v1 whole, which is shorter than its diff:
```python
import functools

import jax
import jax.numpy as jnp
from jax import lax
from jax.experimental import pallas as pl
from jax.experimental.pallas import tpu as pltpu
from jax.sharding import PartitionSpec as P

penalty_weight = 2.0
PAIR = 2
F32 = jnp.float32
BF16 = jnp.bfloat16
MESH = pl.DeviceIdType.MESH


def pack(rows):
    half = rows.shape[-1] // 2
    return jnp.concatenate([rows[..., :half], rows[..., half:]], axis=-2).astype(BF16)


def loop(count, body):
    if count == 1:
        body(0)
    else:
        pl.loop(0, count)(body)


def comm_kernel(
    n, ns, C, HC,
    act, enc_hbm, bias, dec_hbm, dbias,
    loss_out, g_out, lat_out, coef_out,
    x_all, g_all, enc_v, dec_v, part, rs, rs1, rs2s, rs2r, norm, loss_s, loss_m,
    load_sem, xs_sem, xr_sem, gs_sem, gr_sem, ps_sem, pr_sem,
    r1s_sem, r1r_sem, r2s_sem, r2r_sem, ls_sem, lr_sem, ms_sem, mr_sem,
):
    A = n // PAIR
    T = n * 8
    TB = min(n, 8)
    sec = lax.axis_index("section")
    me = lax.axis_index("mp")
    a, b = me // PAIR, lax.rem(me, PAIR)
    ob = 1 - b
    partner = a * PAIR + ob
    half = x_all.shape[2]
    hid = enc_v.shape[1]

    barrier = pltpu.get_barrier_semaphore()
    for k in range(1, n):
        pl.semaphore_signal(barrier, inc=1, device_id={"mp": lax.rem(me + k, n)}, device_id_type=MESH)
    for k in range(1, ns):
        pl.semaphore_signal(barrier, inc=1, device_id={"section": lax.rem(sec + k, ns)}, device_id_type=MESH)

    enc_copy = pltpu.make_async_copy(enc_hbm, enc_v, load_sem.at[0])
    dec_copy = pltpu.make_async_copy(dec_hbm, dec_v, load_sem.at[1])
    enc_copy.start()
    dec_copy.start()

    x_all[me] = pack(act[...].astype(F32))
    pl.semaphore_wait(barrier, n - 1 + ns - 1)

    def remote(src, dst, ssem, rsem, axis, peer):
        return pltpu.make_async_remote_copy(
            src_ref=src, dst_ref=dst, send_sem=ssem, recv_sem=rsem,
            device_id={axis: peer}, device_id_type=MESH,
        )

    def gather_copy(buf, ssem, rsem, slot, index, peer):
        return remote(buf.at[slot], buf.at[slot], ssem.at[index], rsem.at[slot], "mp", peer)

    def gather_start(buf, ssem, rsem):
        copies = []
        for k in range(1, A):
            peer = lax.rem(a + k, A) * PAIR + b
            copies.append(gather_copy(buf, ssem, rsem, me, k - 1, peer))
        copies.append(gather_copy(buf, ssem, rsem, me, A - 1, partner))
        for c in copies[-1:] + copies[:-1]:
            c.start()
        return copies

    def gather_forward(buf, ssem, rsem):
        copies = []
        for k in range(1, A):
            slot = lax.rem(a + A - k, A) * PAIR + b
            c = gather_copy(buf, ssem, rsem, slot, A - 1 + k, partner)
            c.wait_recv()
            c.start()
            copies.append(c)
        return copies

    def gather_finish(buf, ssem, rsem, copies):
        for k in range(A):
            slot = lax.rem(a + A - k, A) * PAIR + ob
            gather_copy(buf, ssem, rsem, slot, 0, partner).wait_recv()
        for c in copies:
            c.wait_send()

    x_copies = gather_start(x_all, xs_sem, xr_sem)
    dec_copy.wait()

    @pl.loop(0, hid // 32)
    def _(i):
        rows = pl.ds(pl.multiple_of(i * 32, 32), 32)
        acc = jnp.zeros((32, 128), F32)
        for k in range(dec_v.shape[1] // 128):
            w = dec_v[rows, k * 128:(k + 1) * 128].astype(F32)
            acc = acc + w * w
        total = jnp.sum(acc, axis=1, keepdims=True)
        norm[rows, :] = jnp.broadcast_to(jnp.sqrt(total + 1e-06), (32, 128))

    x_copies += gather_forward(x_all, xs_sem, xr_sem)
    enc_copy.wait()
    gather_finish(x_all, xs_sem, xr_sem, x_copies)

    hw = hid // HC
    p_copies = []
    for h in range(HC):
        def enc_step(i, h=h):
            blocks = pl.ds(i * TB, TB)
            x = x_all[blocks].reshape(TB * 16, half)
            lo = jnp.dot(x, enc_v[:half, h * hw:(h + 1) * hw], preferred_element_type=F32)
            hi = jnp.dot(x, enc_v[half:, h * hw:(h + 1) * hw], preferred_element_type=F32)
            lo = lo.reshape(TB, 16, hw)[:, :8]
            hi = hi.reshape(TB, 16, hw)[:, 8:]
            rows = pl.ds(pl.multiple_of(i * TB * 8, TB * 8), TB * 8)
            part[h, sec, rows, :] = (lo + hi).reshape(TB * 8, hw).astype(BF16)

        loop(n // TB, enc_step)
        for k in range(1, ns):
            peer = lax.rem(sec + k, ns)
            c = remote(part.at[h, sec], part.at[h, sec], ps_sem.at[h, k - 1], pr_sem.at[h, sec], "section", peer)
            c.start()
            p_copies.append(c)
    for h in range(HC):
        for k in range(1, ns):
            src = lax.rem(sec + k, ns)
            remote(part.at[h, src], part.at[h, src], ps_sem.at[h, k - 1], pr_sem.at[h, src], "section", src).wait_recv()
        cols = slice(h * hw, (h + 1) * hw)

        def lat_step(i, h=h, cols=cols):
            rows = pl.ds(pl.multiple_of(i * TB * 8, TB * 8), TB * 8)
            pre = bias[:, cols]
            for s in range(ns):
                pre = pre + part[h, s, rows, :].astype(F32)
            lat_out[rows, cols] = jnp.maximum(pre, 0.0).astype(BF16)

        loop(n // TB, lat_step)

    cw = half // C

    def block(c, dest):
        return rs.at[c, dest]

    r1_copies = []
    for c in range(C):
        def dec_step(i, c=c):
            rows = pl.ds(pl.multiple_of(i * TB * 8, TB * 8), TB * 8)
            lat = lat_out[rows, :]
            lo = jnp.dot(lat, dec_v[:, c * cw:(c + 1) * cw], preferred_element_type=F32)
            hi = jnp.dot(lat, dec_v[:, half + c * cw:half + (c + 1) * cw], preferred_element_type=F32)
            both = jnp.concatenate([lo.reshape(TB, 8, cw), hi.reshape(TB, 8, cw)], axis=1)
            rs[c, pl.ds(i * TB, TB)] = both.astype(BF16)

        loop(n // TB, dec_step)
        for k in range(1, A + 1):
            row = lax.rem(a + k, A)
            cp = remote(rs.at[c, row * PAIR + ob], rs1.at[c, row], r1s_sem.at[c, k - 1], r1r_sem.at[c, row], "mp", partner)
            cp.start()
            r1_copies.append(cp)

    ones = jnp.ones((T, 128), BF16)
    lat_sum = lax.dot_general(lat_out[...], ones, (((0,), (0,)), ((), ())), preferred_element_type=F32)
    coef_out[...] = penalty_weight * lat_sum / T / norm[...]
    penalty = penalty_weight / T * jnp.sum(lat_sum[:, :1] * norm[:, :1])

    r2_copies = []
    for c in range(C):
        for k in range(1, A):
            row = lax.rem(a + k, A)
            remote(rs.at[c, 0], rs1.at[c, row], r1s_sem.at[c, k - 1], r1r_sem.at[c, row], "mp", partner).wait_recv()
            rs2s[c, row] = (rs[c, row * PAIR + b].astype(F32) + rs1[c, row].astype(F32)).astype(BF16)
            cp = remote(rs2s.at[c, row], rs2r.at[c, a], r2s_sem.at[c, k - 1], r2r_sem.at[c, a], "mp", row * PAIR + b)
            cp.start()
            r2_copies.append(cp)
    squares = jnp.zeros((), F32)
    for c in range(C):
        remote(rs.at[c, 0], rs1.at[c, a], r1s_sem.at[c, A - 1], r1r_sem.at[c, a], "mp", partner).wait_recv()
        total = rs[c, me].astype(F32) + rs1[c, a].astype(F32)
        for k in range(1, A):
            row = lax.rem(a + A - k, A)
            remote(rs2s.at[c, row], rs2r.at[c, row], r2s_sem.at[c, k - 1], r2r_sem.at[c, row], "mp", partner).wait_recv()
            total = total + rs2r[c, row].astype(F32)
        lo = slice(c * cw, (c + 1) * cw)
        hi = slice(half + c * cw, half + (c + 1) * cw)
        own = jnp.concatenate([act[:, lo].astype(F32), act[:, hi].astype(F32)], axis=0)
        shift = jnp.concatenate([jnp.broadcast_to(dbias[:, lo], (8, cw)), jnp.broadcast_to(dbias[:, hi], (8, cw))], axis=0)
        error = total + shift - own
        squares = squares + jnp.sum(error * error)
        g_all[me, :, lo] = (2.0 * error / T).astype(BF16)

    g_copies = gather_start(g_all, gs_sem, gr_sem)
    loss_s[sec] = jnp.full((8, 128), squares / T + penalty, F32)
    l_copies = []
    for k in range(1, ns):
        peer = lax.rem(sec + k, ns)
        cp = remote(loss_s.at[sec], loss_s.at[sec], ls_sem.at[k - 1], lr_sem.at[sec], "section", peer)
        cp.start()
        l_copies.append(cp)
    for cp in p_copies + r1_copies + r2_copies:
        cp.wait_send()
    for k in range(1, ns):
        src = lax.rem(sec + k, ns)
        remote(loss_s.at[src], loss_s.at[src], ls_sem.at[k - 1], lr_sem.at[src], "section", src).wait_recv()
    total = loss_s[0]
    for s in range(1, ns):
        total = total + loss_s[s]
    loss_m[me] = total
    for k in range(1, n):
        peer = lax.rem(me + k, n)
        cp = remote(loss_m.at[me], loss_m.at[me], ms_sem.at[k - 1], mr_sem.at[me], "mp", peer)
        cp.start()
        l_copies.append(cp)
    g_copies += gather_forward(g_all, gs_sem, gr_sem)
    for k in range(1, n):
        src = lax.rem(me + k, n)
        remote(loss_m.at[src], loss_m.at[src], ms_sem.at[k - 1], mr_sem.at[src], "mp", src).wait_recv()
    total = loss_m[0]
    for s in range(1, n):
        total = total + loss_m[s]
    loss_out[...] = total
    gather_finish(g_all, gs_sem, gr_sem, g_copies)

    def out_step(i):
        g_out[pl.ds(i * TB, TB)] = g_all[pl.ds(i * TB, TB)]

    loop(n // TB, out_step)
    for cp in l_copies:
        cp.wait_send()


def grad_kernel(blocks, g, lat, coef, w, out, bias_out, spread):
    step = pl.program_id(0)
    n = g.shape[0]
    per = pl.num_programs(0) // 2

    @pl.when(step == 0)
    def _():
        rows = lat[...].astype(F32).reshape(n, 8, lat.shape[1])
        zero = jnp.zeros_like(rows)
        spread[0] = jnp.concatenate([rows, zero], axis=1).astype(BF16).reshape(n * 16, lat.shape[1])
        spread[1] = jnp.concatenate([zero, rows], axis=1).astype(BF16).reshape(n * 16, lat.shape[1])

    side = step // per
    cw = out.shape[1]
    cols = pl.ds(pl.multiple_of(lax.rem(step, per) * cw, cw), cw)
    gb = g[:, :, cols]
    sides = jnp.sum(gb.astype(F32), axis=0)
    lo = jnp.sum(sides[:8], axis=0, keepdims=True)
    hi = jnp.sum(sides[8:], axis=0, keepdims=True)
    bias_out[...] = jnp.where(side == 0, lo, hi)
    total = lax.dot_general(
        spread[side], gb.reshape(n * 16, cw), (((0,), (0,)), ((), ())), preferred_element_type=F32
    )
    out[...] = (total + coef[:, :1] * w[...].astype(F32)).astype(BF16)


def local(ns, n, activations, enc_weight, enc_bias, dec_weight, dec_bias):
    act = activations[0]
    enc = enc_weight[0]
    w_dec = dec_weight[:, 0, :]
    rows, d = act.shape
    hid = enc.shape[1]
    T = rows * n
    half = d // 2
    A = n // PAIR
    C, HC = 2, 2
    vmem = pl.BlockSpec(memory_space=pltpu.VMEM)
    anys = pl.BlockSpec(memory_space=pl.ANY)
    dma = pltpu.SemaphoreType.DMA
    loss, g, lat, coef = pl.pallas_call(
        functools.partial(comm_kernel, n, ns, C, HC),
        out_shape=(
            jax.ShapeDtypeStruct((8, 128), F32),
            jax.ShapeDtypeStruct((n, 16, half), BF16),
            jax.ShapeDtypeStruct((T, hid), BF16),
            jax.ShapeDtypeStruct((hid, 128), F32),
        ),
        in_specs=[vmem, anys, vmem, anys, vmem],
        out_specs=[vmem] * 4,
        scratch_shapes=[
            pltpu.VMEM((n, 16, half), BF16),
            pltpu.VMEM((n, 16, half), BF16),
            pltpu.VMEM((d, hid), BF16),
            pltpu.VMEM((hid, d), BF16),
            pltpu.VMEM((HC, ns, T, hid // HC), BF16),
            pltpu.VMEM((C, n, 16, half // C), BF16),
            pltpu.VMEM((C, A, 16, half // C), BF16),
            pltpu.VMEM((C, A, 16, half // C), BF16),
            pltpu.VMEM((C, A, 16, half // C), BF16),
            pltpu.VMEM((hid, 128), F32),
            pltpu.VMEM((ns, 8, 128), F32),
            pltpu.VMEM((n, 8, 128), F32),
            dma((2,)),
            dma((2 * A,)), dma((n,)),
            dma((2 * A,)), dma((n,)),
            dma((HC, ns)), dma((HC, ns)),
            dma((C, A)), dma((C, A)),
            dma((C, A)), dma((C, A)),
            dma((ns,)), dma((ns,)),
            dma((n,)), dma((n,)),
        ],
        compiler_params=pltpu.CompilerParams(
            collective_id=0, has_side_effects=True, vmem_limit_bytes=48 * 1024 * 1024
        ),
        name="crosscoder_comm",
    )(act, enc, enc_bias[None, :], w_dec, dec_bias)

    steps = 8
    cw = d // steps
    grad_dec, bias_sum = pl.pallas_call(
        functools.partial(grad_kernel, steps),
        grid=(steps,),
        out_shape=(
            jax.ShapeDtypeStruct((hid, d), BF16),
            jax.ShapeDtypeStruct((1, d), F32),
        ),
        in_specs=[vmem, vmem, vmem, pl.BlockSpec((hid, cw), lambda i: (0, i))],
        out_specs=[pl.BlockSpec((hid, cw), lambda i: (0, i)), pl.BlockSpec((1, cw), lambda i: (0, i))],
        scratch_shapes=[pltpu.VMEM((2, n * 16, hid), BF16)],
        name="grad_dec",
    )(g, lat, coef, w_dec)
    width = d // n
    grad_bias = lax.dynamic_slice_in_dim(bias_sum, lax.axis_index("mp") * width, width, 1)
    return loss[0, 0], grad_dec[:, None, :], grad_bias


def solution(mesh):
    in_specs = (
        P("section", "mp", None),
        P("section", None, "mp"),
        P("mp"),
        P("mp", "section", None),
        P("section", None),
    )
    out_specs = (P(), P("mp", "section", None), P("section", "mp"))
    body = functools.partial(local, mesh.shape["section"], mesh.shape["mp"])
    return jax.shard_map(body, mesh=mesh, in_specs=in_specs, out_specs=out_specs, check_vma=False)
```

time: 231 us -> 60.3 us (0.26)
  blocking collectives: 110 us -> 0 us
  waiting for transfers between devices: 87 us -> 0 us
  Pallas kernels: 0 us -> 50.8 us
  between operations: 15.4 us -> 0.66 us
  matrix products: 13.2 us -> 0 us
  local copies, waits for them, and re-layouts: 0.03 us -> 8.31 us
  other arithmetic: 5.29 us -> 0 us
    all_gather x2 -> x0, blocking collectives: 64.5 us -> none  [the longest x1 33.2 us: local(): all_rows = lax.all_gather(activations[0], 'mp', axis=0, tiled=True)]
    reduce_scatter x1 -> x0, waiting for transfers between devices: 54.2 us -> none  [local(): lax.psum_scatter(lax.dot_general(w_dec, latents, (((0,), (1,)), ((), ()))...]
    pallas_call x0 -> x2, Pallas kernels: none -> 50.8 us  [the longest x1 43 us: local(): pl.pallas_call(functools.partial(comm_kernel, n, ns, C, HC), out_shape=(j...]
    psum x2 -> x0, blocking collectives: 45.6 us -> none  [the longest x1 39.8 us: local(): loss = lax.psum(square_sum / token_count + penalty_part, ('section', 'mp'))]
    psum x1 -> x0, waiting for transfers between devices: 32.7 us -> none  [local(): lax.psum(partial_value.astype(jnp.bfloat16), 'section').astype(jnp.float32)]
    dot_general x3 -> x0, matrix products: 13.2 us -> none  [the longest x1 5.49 us: local(): lax.dot_general(latents, lax.all_gather(grad_rec_t, 'mp', axis=0, tiled=T...]
    unnamed x6 -> x14, local copies, waits for them, and re-layouts: 0.02 us -> 6.55 us
    reduce_sum x3 -> x0, other arithmetic: 5.27 us -> none  [the longest x1 3.08 us: local(): jnp.sum(jnp.square(w_dec.astype(jnp.float32)), axis=1) + 1e-06]
  transfers between devices with their start and end apart: 2 -> 0, of which waited for: 2 -> 0; matrix products, arithmetic and copies ran while one was open for 2% -> 0% of each run, Pallas kernels for 0% -> 0%
where the time goes in v1:
time: 60.3 us; the launch traced here: 59.8 us
  Pallas kernels  50.8 us (84%)
  local copies, waits for them, and re-layouts  8.31 us (14%)
  between operations  0.66 us (1%)
    pallas_call x1, Pallas kernels, local(): pl.pallas_call(functools.partial(comm_kernel, n, ns, C, HC), out_shape=(j...  43 us
    pallas_call x1, Pallas kernels, local(): pl.pallas_call(functools.partial(grad_kernel, steps), grid=(steps,), out_...  7.84 us
    unnamed x14, local copies, waits for them, and re-layouts  6.55 us
    dynamic_slice x1, local copies, waits for them, and re-layouts, local(): lax.dynamic_slice_in_dim(bias_sum, lax.axis_index('mp') * width, width, 1)  1.25 us

profile of v1, /device:TPU:0, one launch (start us, length us, event | category | flops | bytes accessed | tf_op | source)
XLA Modules:
  0.0 59.8 jit_solution(405481258713660406)
XLA Ops:
  0.6 0.0 copy-start
  0.6 2.2 %copy-done = bf16[1,4096,512]{2,1,0:T(8,128)(2,1)S(1)} copy-done((bf16[1,4096,512]{2,1,0:T(8,128)(2,1)S(1)}, bf16[1,4096,512]{2,1,0:T(8,128)(2,1)}, u32[]{:S(2)}) %copy-start) | copy-done | bytes 4194328
  2.8 0.0 copy-start.3
  2.8 0.8 %copy-done.3 = bf16[1,8,4096]{2,1,0:T(8,128)(2,1)S(1)} copy-done((bf16[1,8,4096]{2,1,0:T(8,128)(2,1)S(1)}, bf16[1,8,4096]{2,1,0:T(8,128)(2,1)}, u32[]{:S(2)}) %copy-start.3) | copy-done | bytes 65560
  3.7 0.0 copy-start.5
  3.7 0.7 %copy-done.5 = f32[1,4096]{1,0:T(1,128)S(1)} copy-done((f32[1,4096]{1,0:T(1,128)S(1)}, f32[1,4096]{1,0:T(1,128)}, u32[]{:S(2)}) %copy-start.5) | copy-done | bytes 16408
  4.4 0.0 copy-start.6
  4.4 0.7 %copy-done.6 = f32[512]{0:T(512)S(1)} copy-done((f32[512]{0:T(512)S(1)}, f32[512]{0:T(512)}, u32[]{:S(2)}) %copy-start.6) | copy-done | bytes 2072
  5.1 43.0 %crosscoder_comm.1 = (f32[8,128]{1,0:T(8,128)S(1)}, bf16[8,16,2048]{2,1,0:T(8,128)(2,1)S(1)}, bf16[64,512]{1,0:T(8,128)(2,1)S(1)}, f32[512,128]{1,0:T(8,128)S(1)}) custom-call(bf16[8,4096]{1,0:T(8,128)(2,1)S(1)} %bitcast.7, bf16[4096,512]{1,0:T(8,128)(2,1)S(1)} %bitcast.6, f32[1,512]{1,0:T(1,128)S(1)} %bitcast.8, bf16[512,4096]{1,0:T(8,128)(2,1)} %bitcast.9, ...), custom_call_target="tpu_custom_call" | custom-call | tf_op jit(solution)/shard_map/crosscoder_comm/pallas_call | solution.py:280
  48.1 0.0 copy-start.1
  48.1 0.8 %copy-done.1 = bf16[8,16,2048]{2,1,0:T(8,128)(2,1)} copy-done((bf16[8,16,2048]{2,1,0:T(8,128)(2,1)}, bf16[8,16,2048]{2,1,0:T(8,128)(2,1)S(1)}, u32[]{:S(2)}) %copy-start.1) | copy-done | bytes 524312
  48.9 0.0 copy-start.2
  48.9 0.7 %copy-done.2 = f32[512,128]{1,0:T(8,128)} copy-done((f32[512,128]{1,0:T(8,128)}, f32[512,128]{1,0:T(8,128)S(1)}, u32[]{:S(2)}) %copy-start.2) | copy-done | bytes 262168
  49.6 0.0 copy-start.4
  49.6 0.6 %copy-done.4 = bf16[64,512]{1,0:T(8,128)(2,1)} copy-done((bf16[64,512]{1,0:T(8,128)(2,1)}, bf16[64,512]{1,0:T(8,128)(2,1)S(1)}, u32[]{:S(2)}) %copy-start.4) | copy-done | bytes 65560
  50.2 0.5 slice.3
  50.7 7.8 %grad_dec.1 = (bf16[512,4096]{1,0:T(8,128)(2,1)}, f32[1,4096]{1,0:T(1,128)}) custom-call(bf16[8,16,2048]{2,1,0:T(8,128)(2,1)} %copy-done.1, bf16[64,512]{1,0:T(8,128)(2,1)} %copy-done.4, f32[512,128]{1,0:T(8,128)} %copy-done.2, bf16[512,4096]{1,0:T(8,128)(2,1)} %bitcast.10), custom_call_target="tpu_custom_call" | custom-call | tf_op jit(solution)/shard_map/grad_dec/pallas_call | solution.py:320
  58.6 1.3 %constant_dynamic-slice_fusion = f32[1,512]{1,0:T(1,128)} fusion(f32[1,4096]{1,0:T(1,128)} %get-tuple-element.14, s32[]{:T(128)S(6)} %select_n.3), kind=kLoop, calls=%fused_computation | loop fusion | bytes 4100 | tf_op jit(solution)/shard_map/dynamic_slice | solution.py:333
Async XLA Ops:
  0.6 2.2 %copy-start = (bf16[1,4096,512]{2,1,0:T(8,128)(2,1)S(1)}, bf16[1,4096,512]{2,1,0:T(8,128)(2,1)}, u32[]{:S(2)}) copy-start(bf16[1,4096,512]{2,1,0:T(8,128)(2,1)} %param.6) | copy-start | bytes 12582916
  2.8 0.8 %copy-start.3 = (bf16[1,8,4096]{2,1,0:T(8,128)(2,1)S(1)}, bf16[1,8,4096]{2,1,0:T(8,128)(2,1)}, u32[]{:S(2)}) copy-start(bf16[1,8,4096]{2,1,0:T(8,128)(2,1)} %param.5) | copy-start | bytes 196612
  3.7 0.7 %copy-start.5 = (f32[1,4096]{1,0:T(1,128)S(1)}, f32[1,4096]{1,0:T(1,128)}, u32[]{:S(2)}) copy-start(f32[1,4096]{1,0:T(1,128)} %dbias.1) | copy-start | bytes 49156
  4.4 0.7 %copy-start.6 = (f32[512]{0:T(512)S(1)}, f32[512]{0:T(512)}, u32[]{:S(2)}) copy-start(f32[512]{0:T(512)} %param.7) | copy-start | bytes 6148
  48.1 0.8 %copy-start.1 = (bf16[8,16,2048]{2,1,0:T(8,128)(2,1)}, bf16[8,16,2048]{2,1,0:T(8,128)(2,1)S(1)}, u32[]{:S(2)}) copy-start(bf16[8,16,2048]{2,1,0:T(8,128)(2,1)S(1)} %get-tuple-element.10.g) | copy-start | bytes 1572868
  48.9 0.7 %copy-start.2 = (f32[512,128]{1,0:T(8,128)}, f32[512,128]{1,0:T(8,128)S(1)}, u32[]{:S(2)}) copy-start(f32[512,128]{1,0:T(8,128)S(1)} %get-tuple-element.12.coef) | copy-start | bytes 786436
  49.6 0.6 %copy-start.4 = (bf16[64,512]{1,0:T(8,128)(2,1)}, bf16[64,512]{1,0:T(8,128)(2,1)S(1)}, u32[]{:S(2)}) copy-start(bf16[64,512]{1,0:T(8,128)(2,1)S(1)} %get-tuple-element.11.lat) | copy-start | bytes 196612

commit v2 on v1

--- a/solution.py
+++ b/solution.py
@@ -9,6 +9,7 @@
 
 penalty_weight = 2.0
 PAIR = 2
+STEPS = 8
 F32 = jnp.float32
 BF16 = jnp.bfloat16
 MESH = pl.DeviceIdType.MESH
@@ -28,9 +29,9 @@
 
 def comm_kernel(
     n, ns, C, HC,
-    act, enc_hbm, bias, dec_hbm, dbias,
-    loss_out, g_out, lat_out, coef_out,
-    x_all, g_all, enc_v, dec_v, part, rs, rs1, rs2s, rs2r, norm, loss_s, loss_m,
+    act_hbm, enc_hbm, bias_hbm, dec_hbm, dbias_hbm,
+    loss_out, g_out, spread_out, coef_out,
+    act, bias, dbias, lat_out, x_all, g_all, enc_v, dec_v, part, rs, rs1, rs2s, rs2r, norm, loss_s, loss_m,
     load_sem, xs_sem, xr_sem, gs_sem, gr_sem, ps_sem, pr_sem,
     r1s_sem, r1r_sem, r2s_sem, r2r_sem, ls_sem, lr_sem, ms_sem, mr_sem,
 ):
@@ -51,10 +52,14 @@
     for k in range(1, ns):
         pl.semaphore_signal(barrier, inc=1, device_id={"section": lax.rem(sec + k, ns)}, device_id_type=MESH)
 
-    enc_copy = pltpu.make_async_copy(enc_hbm, enc_v, load_sem.at[0])
-    dec_copy = pltpu.make_async_copy(dec_hbm, dec_v, load_sem.at[1])
-    enc_copy.start()
-    dec_copy.start()
+    act_copy = pltpu.make_async_copy(act_hbm, act, load_sem.at[0])
+    enc_copy = pltpu.make_async_copy(enc_hbm, enc_v, load_sem.at[1])
+    dec_copy = pltpu.make_async_copy(dec_hbm, dec_v, load_sem.at[2])
+    bias_copy = pltpu.make_async_copy(bias_hbm, bias, load_sem.at[3])
+    dbias_copy = pltpu.make_async_copy(dbias_hbm, dbias, load_sem.at[4])
+    for c in (act_copy, dec_copy, enc_copy, bias_copy, dbias_copy):
+        c.start()
+    act_copy.wait()
 
     x_all[me] = pack(act[...].astype(F32))
     pl.semaphore_wait(barrier, n - 1 + ns - 1)
@@ -109,7 +114,8 @@
         norm[rows, :] = jnp.broadcast_to(jnp.sqrt(total + 1e-06), (32, 128))
 
     x_copies += gather_forward(x_all, xs_sem, xr_sem)
-    enc_copy.wait()
+    for c in (enc_copy, bias_copy, dbias_copy):
+        c.wait()
     gather_finish(x_all, xs_sem, xr_sem, x_copies)
 
     hw = hid // HC
@@ -221,6 +227,11 @@
         cp.start()
         l_copies.append(cp)
     g_copies += gather_forward(g_all, gs_sem, gr_sem)
+    wide = lat_out[...].astype(F32).reshape(n, 8, hid)
+    zero = jnp.zeros_like(wide)
+    spread_out[0] = jnp.concatenate([wide, zero], axis=1).reshape(n * 16, hid).T.astype(BF16)
+    spread_out[1] = jnp.concatenate([zero, wide], axis=1).reshape(n * 16, hid).T.astype(BF16)
+
     for k in range(1, n):
         src = lax.rem(me + k, n)
         remote(loss_m.at[src], loss_m.at[src], ms_sem.at[k - 1], mr_sem.at[src], "mp", src).wait_recv()
@@ -238,30 +249,36 @@
         cp.wait_send()
 
 
-def grad_kernel(blocks, g, lat, coef, w, out, bias_out, spread):
+def grad_kernel(loss, g, spread, coef, w, loss_out, out, bias_out):
     step = pl.program_id(0)
     n = g.shape[0]
     per = pl.num_programs(0) // 2
+    hid, cw = out.shape
 
     @pl.when(step == 0)
     def _():
-        rows = lat[...].astype(F32).reshape(n, 8, lat.shape[1])
-        zero = jnp.zeros_like(rows)
-        spread[0] = jnp.concatenate([rows, zero], axis=1).astype(BF16).reshape(n * 16, lat.shape[1])
-        spread[1] = jnp.concatenate([zero, rows], axis=1).astype(BF16).reshape(n * 16, lat.shape[1])
+        loss_out[...] = loss[:1, :1]
 
     side = step // per
-    cw = out.shape[1]
     cols = pl.ds(pl.multiple_of(lax.rem(step, per) * cw, cw), cw)
     gb = g[:, :, cols]
-    sides = jnp.sum(gb.astype(F32), axis=0)
-    lo = jnp.sum(sides[:8], axis=0, keepdims=True)
-    hi = jnp.sum(sides[8:], axis=0, keepdims=True)
-    bias_out[...] = jnp.where(side == 0, lo, hi)
-    total = lax.dot_general(
-        spread[side], gb.reshape(n * 16, cw), (((0,), (0,)), ((), ())), preferred_element_type=F32
-    )
-    out[...] = (total + coef[:, :1] * w[...].astype(F32)).astype(BF16)
+
+    def bias_step():
+        sums = jnp.sum(gb.astype(F32), axis=0)
+        lo = jnp.sum(sums[:8], axis=0, keepdims=True)
+        hi = jnp.sum(sums[8:], axis=0, keepdims=True)
+        bias_out[...] = jnp.where(side == 0, lo, hi)
+
+    if bias_out.shape[1] == cw and STEPS == n:
+        pl.when(step == lax.axis_index("mp"))(bias_step)
+    else:
+        bias_step()
+    gm = gb.reshape(n * 16, cw)
+    wcols = pl.ds(pl.multiple_of(step * cw, cw), cw)
+    for r in range(0, hid, 128):
+        total = jnp.dot(spread[side, r:r + 128, :], gm, preferred_element_type=F32)
+        scale = jnp.concatenate([coef[r:r + 128, :]] * (cw // 128), axis=1)
+        out[r:r + 128, :] = (total + scale * w[r:r + 128, wcols].astype(F32)).astype(BF16)
 
 
 def local(ns, n, activations, enc_weight, enc_bias, dec_weight, dec_bias):
@@ -275,19 +292,23 @@
     A = n // PAIR
     C, HC = 2, 2
     vmem = pl.BlockSpec(memory_space=pltpu.VMEM)
-    anys = pl.BlockSpec(memory_space=pl.ANY)
+    hbm = pl.BlockSpec(memory_space=pltpu.HBM)
     dma = pltpu.SemaphoreType.DMA
-    loss, g, lat, coef = pl.pallas_call(
+    loss, g, spread, coef = pl.pallas_call(
         functools.partial(comm_kernel, n, ns, C, HC),
         out_shape=(
             jax.ShapeDtypeStruct((8, 128), F32),
             jax.ShapeDtypeStruct((n, 16, half), BF16),
-            jax.ShapeDtypeStruct((T, hid), BF16),
+            jax.ShapeDtypeStruct((2, hid, n * 16), BF16),
             jax.ShapeDtypeStruct((hid, 128), F32),
         ),
-        in_specs=[vmem, anys, vmem, anys, vmem],
+        in_specs=[hbm] * 5,
         out_specs=[vmem] * 4,
         scratch_shapes=[
+            pltpu.VMEM((rows, d), BF16),
+            pltpu.VMEM((1, hid), F32),
+            pltpu.VMEM((1, d), F32),
+            pltpu.VMEM((T, hid), BF16),
             pltpu.VMEM((n, 16, half), BF16),
             pltpu.VMEM((n, 16, half), BF16),
             pltpu.VMEM((d, hid), BF16),
@@ -300,7 +321,7 @@
             pltpu.VMEM((hid, 128), F32),
             pltpu.VMEM((ns, 8, 128), F32),
             pltpu.VMEM((n, 8, 128), F32),
-            dma((2,)),
+            dma((5,)),
             dma((2 * A,)), dma((n,)),
             dma((2 * A,)), dma((n,)),
             dma((HC, ns)), dma((HC, ns)),
@@ -310,28 +331,34 @@
             dma((n,)), dma((n,)),
         ],
         compiler_params=pltpu.CompilerParams(
-            collective_id=0, has_side_effects=True, vmem_limit_bytes=48 * 1024 * 1024
+            collective_id=0, has_side_effects=True, vmem_limit_bytes=(28 + n // 4) * 1024 * 1024
         ),
         name="crosscoder_comm",
-    )(act, enc, enc_bias[None, :], w_dec, dec_bias)
-
-    steps = 8
-    cw = d // steps
-    grad_dec, bias_sum = pl.pallas_call(
-        functools.partial(grad_kernel, steps),
+    )(*(pltpu.with_memory_space_constraint(v, pltpu.HBM) for v in (act, enc, enc_bias[None, :], w_dec, dec_bias)))
+
+    steps = STEPS
+    cw, width = d // steps, d // n
+    own = steps == n
+    loss, grad_dec, bias = pl.pallas_call(
+        grad_kernel,
         grid=(steps,),
         out_shape=(
+            jax.ShapeDtypeStruct((1, 1), F32),
             jax.ShapeDtypeStruct((hid, d), BF16),
-            jax.ShapeDtypeStruct((1, d), F32),
+            jax.ShapeDtypeStruct((1, width if own else d), F32),
         ),
-        in_specs=[vmem, vmem, vmem, pl.BlockSpec((hid, cw), lambda i: (0, i))],
-        out_specs=[pl.BlockSpec((hid, cw), lambda i: (0, i)), pl.BlockSpec((1, cw), lambda i: (0, i))],
-        scratch_shapes=[pltpu.VMEM((2, n * 16, hid), BF16)],
+        in_specs=[vmem] * 5,
+        out_specs=[
+            pl.BlockSpec((1, 1), lambda i: (0, 0)),
+            pl.BlockSpec((hid, cw), lambda i: (0, i)),
+            pl.BlockSpec((1, cw), lambda i: (0, 0) if own else (0, i)),
+        ],
+        compiler_params=pltpu.CompilerParams(vmem_limit_bytes=18 * 1024 * 1024),
         name="grad_dec",
-    )(g, lat, coef, w_dec)
-    width = d // n
-    grad_bias = lax.dynamic_slice_in_dim(bias_sum, lax.axis_index("mp") * width, width, 1)
-    return loss[0, 0], grad_dec[:, None, :], grad_bias
+    )(loss, g, spread, coef, w_dec)
+    if not own:
+        bias = lax.dynamic_slice_in_dim(bias, lax.axis_index("mp") * width, width, 1)
+    return loss.reshape(()), grad_dec[:, None, :], bias
 
 
 def solution(mesh):

time: 60.3 us -> 48.7 us (0.81)
  local copies, waits for them, and re-layouts: 8.31 us -> 0.01 us
  Pallas kernels: 50.8 us -> 47.9 us
    unnamed x14 -> x2, local copies, waits for them, and re-layouts: 6.55 us -> 0.01 us
    pallas_call x1, Pallas kernels: 7.84 us -> 4.75 us  [local(): pl.pallas_call(grad_kernel, grid=(steps,), out_shape=(jax.ShapeDtypeStruc...]
    dynamic_slice x1 -> x0, local copies, waits for them, and re-layouts: 1.25 us -> none  [local(): lax.dynamic_slice_in_dim(bias_sum, lax.axis_index('mp') * width, width, 1)]
where the time goes in v2:
time: 48.7 us; the launch traced here: 48.5 us
  Pallas kernels  47.9 us (98%)
  between operations  0.66 us (1%)
    pallas_call x1, Pallas kernels, local(): pl.pallas_call(functools.partial(comm_kernel, n, ns, C, HC), out_shape=(j...  43.1 us
    pallas_call x1, Pallas kernels, local(): pl.pallas_call(grad_kernel, grid=(steps,), out_shape=(jax.ShapeDtypeStruc...  4.75 us

profile of v2, /device:TPU:0, one launch (start us, length us, event | category | flops | bytes accessed | tf_op | source)
XLA Modules:
  0.0 48.5 jit_solution(17869710060493492327)
XLA Ops:
  0.6 0.0 copy-start
  0.6 43.1 %crosscoder_comm.1 = (f32[8,128]{1,0:T(8,128)S(1)}, bf16[8,16,2048]{2,1,0:T(8,128)(2,1)S(1)}, bf16[2,512,128]{2,1,0:T(8,128)(2,1)S(1)}, f32[512,128]{1,0:T(8,128)S(1)}) custom-call(bf16[8,4096]{1,0:T(8,128)(2,1)} %bitcast.9, bf16[4096,512]{1,0:T(8,128)(2,1)} %bitcast.8, f32[1,512]{1,0:T(1,128)} %bitcast.10, bf16[512,4096]{1,0:T(8,128)(2,1)} %bitcast.6, ...), custom_call_target="tpu_custom_call" | custom-call | tf_op jit(solution)/shard_map/crosscoder_comm/pallas_call | solution.py:297
  43.8 0.0 copy-done
  43.8 4.7 %grad_dec.1 = (f32[1,1]{1,0:T(1,128)}, bf16[512,4096]{1,0:T(8,128)(2,1)}, f32[1,512]{1,0:T(1,128)}) custom-call(f32[8,128]{1,0:T(8,128)S(1)} %get-tuple-element.10.loss, bf16[8,16,2048]{2,1,0:T(8,128)(2,1)S(1)} %get-tuple-element.11.g, bf16[2,512,128]{2,1,0:T(8,128)(2,1)S(1)} %get-tuple-element.12.spread, f32[512,128]{1,0:T(8,128)S(1)} %get-tuple-element.13.coef, ...), custom_call_target="tpu_custom_call" | custom-call | tf_op jit(solution)/shard_map/grad_dec/pallas_call | solution.py:342
Async XLA Ops:
  0.6 43.1 %copy-start = (bf16[512,1,4096]{2,0,1:T(8,128)(2,1)S(1)}, bf16[512,1,4096]{2,0,1:T(8,128)(2,1)}, u32[]{:S(2)}) copy-start(bf16[512,1,4096]{2,0,1:T(8,128)(2,1)} %param.8) | copy-start | bytes 12582916

commit v3 on v2

v3 whole, which is shorter than its diff:
```python
import functools

import jax
import jax.numpy as jnp
from jax import lax
from jax.experimental import pallas as pl
from jax.experimental.pallas import tpu as pltpu
from jax.sharding import PartitionSpec as P

penalty_weight = 2.0
PAIR = 2
F32 = jnp.float32
BF16 = jnp.bfloat16
MESH = pl.DeviceIdType.MESH


def loop(count, body):
    if count == 1:
        body(0)
    else:
        pl.loop(0, count)(body)


def comm_kernel(
    n, ns, C, HC,
    act_hbm, enc_hbm, bias_hbm, dec_hbm, dbias_hbm,
    loss_out, g_out, spread_out, coef_out, first_out, sums_out,
    act, bias, dbias, lat_out, x_all, g_all, enc_v, dec_v, acc_v, part, rs, rs1, rs2s, rs2r, norm, loss_s, loss_m,
    load_sem, xs_sem, xr_sem, gs_sem, gr_sem, ps_sem, pr_sem,
    r1s_sem, r1r_sem, r2s_sem, r2r_sem, ls_sem, lr_sem, ms_sem, mr_sem,
):
    A = n // PAIR
    T = n * 8
    TB = min(n, 8)
    sec = lax.axis_index("section")
    me = lax.axis_index("mp")
    a, b = me // PAIR, lax.rem(me, PAIR)
    ob = 1 - b
    partner = a * PAIR + ob
    half = dec_v.shape[1] // 2
    cw = half // C
    hid = enc_v.shape[1]

    barrier = pltpu.get_barrier_semaphore()
    for k in range(1, n):
        pl.semaphore_signal(barrier, inc=1, device_id={"mp": lax.rem(me + k, n)}, device_id_type=MESH)
    for k in range(1, ns):
        pl.semaphore_signal(barrier, inc=1, device_id={"section": lax.rem(sec + k, ns)}, device_id_type=MESH)

    act_copy = pltpu.make_async_copy(act_hbm, act, load_sem.at[0])
    enc_copy = pltpu.make_async_copy(enc_hbm, enc_v, load_sem.at[1])
    dec_copy = pltpu.make_async_copy(dec_hbm, dec_v, load_sem.at[2])
    bias_copy = pltpu.make_async_copy(bias_hbm, bias, load_sem.at[3])
    dbias_copy = pltpu.make_async_copy(dbias_hbm, dbias, load_sem.at[4])
    for c in (act_copy, dec_copy, enc_copy, bias_copy, dbias_copy):
        c.start()
    act_copy.wait()

    def cols_of(c):
        return slice(c * cw, (c + 1) * cw), slice(half + c * cw, half + (c + 1) * cw)

    for c in range(C):
        lo, hi = cols_of(c)
        x_all[c, me] = jnp.concatenate([act[:, lo].astype(F32), act[:, hi].astype(F32)], axis=0).astype(BF16)
    pl.semaphore_wait(barrier, n - 1 + ns - 1)

    def remote(src, dst, ssem, rsem, axis, peer):
        return pltpu.make_async_remote_copy(
            src_ref=src, dst_ref=dst, send_sem=ssem, recv_sem=rsem,
            device_id={axis: peer}, device_id_type=MESH,
        )

    def gather_copy(buf, ssem, rsem, c, slot, index, peer):
        return remote(buf.at[c, slot], buf.at[c, slot], ssem.at[c, index], rsem.at[c, slot], "mp", peer)

    def gather_start(buf, ssem, rsem, c):
        copies = [gather_copy(buf, ssem, rsem, c, me, A - 1, partner)]
        for k in range(1, A):
            peer = lax.rem(a + k, A) * PAIR + b
            copies.append(gather_copy(buf, ssem, rsem, c, me, k - 1, peer))
        for cp in copies:
            cp.start()
        return copies

    def gather_forward(buf, ssem, rsem, c):
        copies = []
        for k in range(1, A):
            slot = lax.rem(a + A - k, A) * PAIR + b
            cp = gather_copy(buf, ssem, rsem, c, slot, A - 1 + k, partner)
            cp.wait_recv()
            cp.start()
            copies.append(cp)
        return copies

    def gather_finish(buf, ssem, rsem, c):
        for k in range(A):
            slot = lax.rem(a + A - k, A) * PAIR + ob
            gather_copy(buf, ssem, rsem, c, slot, 0, partner).wait_recv()

    x_copies = []
    for c in range(C):
        x_copies += gather_start(x_all, xs_sem, xr_sem, c)
    dec_copy.wait()

    @pl.loop(0, hid // 32)
    def _(i):
        rows = pl.ds(pl.multiple_of(i * 32, 32), 32)
        acc = jnp.zeros((32, 128), F32)
        for k in range(dec_v.shape[1] // 128):
            w = dec_v[rows, k * 128:(k + 1) * 128].astype(F32)
            acc = acc + w * w
        total = jnp.sum(acc, axis=1, keepdims=True)
        norm[rows, :] = jnp.broadcast_to(jnp.sqrt(total + 1e-06), (32, 128))

    for c in range(C):
        x_copies += gather_forward(x_all, xs_sem, xr_sem, c)
    for cp in (enc_copy, bias_copy, dbias_copy):
        cp.wait()

    def enc_chunk(c, i, cols):
        lo, hi = cols_of(c)
        x = x_all[c, pl.ds(i * TB, TB)].reshape(TB * 16, cw)
        left = jnp.dot(x, enc_v[lo, cols], preferred_element_type=F32)
        right = jnp.dot(x, enc_v[hi, cols], preferred_element_type=F32)
        left = left.reshape(TB, 16, left.shape[1])[:, :8]
        right = right.reshape(TB, 16, right.shape[1])[:, 8:]
        return (left + right).reshape(TB * 8, left.shape[2])

    def rows_of(i):
        return pl.ds(pl.multiple_of(i * TB * 8, TB * 8), TB * 8)

    for c in range(C - 1):
        gather_finish(x_all, xs_sem, xr_sem, c)

        def early(i, c=c):
            value = enc_chunk(c, i, slice(0, hid))
            acc_v[rows_of(i), :] = value if c == 0 else acc_v[rows_of(i), :] + value

        loop(n // TB, early)
    gather_finish(x_all, xs_sem, xr_sem, C - 1)

    hw = hid // HC
    p_copies = []
    for h in range(HC):
        def enc_step(i, h=h):
            cols = slice(h * hw, (h + 1) * hw)
            value = acc_v[rows_of(i), cols] + enc_chunk(C - 1, i, cols)
            part[h, sec, rows_of(i), :] = value.astype(BF16)

        loop(n // TB, enc_step)
        for k in range(1, ns):
            peer = lax.rem(sec + k, ns)
            c = remote(part.at[h, sec], part.at[h, sec], ps_sem.at[h, k - 1], pr_sem.at[h, sec], "section", peer)
            c.start()
            p_copies.append(c)
    for h in range(HC):
        for k in range(1, ns):
            src = lax.rem(sec + k, ns)
            remote(part.at[h, src], part.at[h, src], ps_sem.at[h, k - 1], pr_sem.at[h, src], "section", src).wait_recv()
        cols = slice(h * hw, (h + 1) * hw)

        def lat_step(i, h=h, cols=cols):
            rows = pl.ds(pl.multiple_of(i * TB * 8, TB * 8), TB * 8)
            pre = bias[:, cols]
            for s in range(ns):
                pre = pre + part[h, s, rows, :].astype(F32)
            lat_out[rows, cols] = jnp.maximum(pre, 0.0).astype(BF16)

        loop(n // TB, lat_step)

    def r1_start(c, k):
        row = lax.rem(a + k, A)
        cp = remote(rs.at[c, row * PAIR + ob], rs1.at[c, row], r1s_sem.at[c, k - 1], r1r_sem.at[c, row], "mp", partner)
        cp.start()
        return cp

    r1_copies = []
    for c in range(C):
        def dec_step(i, c=c):
            rows = pl.ds(pl.multiple_of(i * TB * 8, TB * 8), TB * 8)
            lat = lat_out[rows, :]
            lo = jnp.dot(lat, dec_v[:, c * cw:(c + 1) * cw], preferred_element_type=F32)
            hi = jnp.dot(lat, dec_v[:, half + c * cw:half + (c + 1) * cw], preferred_element_type=F32)
            both = jnp.concatenate([lo.reshape(TB, 8, cw), hi.reshape(TB, 8, cw)], axis=1)
            rs[c, pl.ds(i * TB, TB)] = both.astype(BF16)

        loop(n // TB, dec_step)
        for k in range(1, A):
            r1_copies.append(r1_start(c, k))
    for c in range(C):
        r1_copies.append(r1_start(c, A))

    ones = jnp.ones((T, 128), BF16)
    lat_sum = lax.dot_general(lat_out[...], ones, (((0,), (0,)), ((), ())), preferred_element_type=F32)
    coef_out[...] = penalty_weight * lat_sum / T / norm[...]
    penalty = penalty_weight / T * jnp.sum(lat_sum[:, :1] * norm[:, :1])

    r2_copies = []
    for c in range(C):
        for k in range(1, A):
            row = lax.rem(a + k, A)
            remote(rs.at[c, 0], rs1.at[c, row], r1s_sem.at[c, k - 1], r1r_sem.at[c, row], "mp", partner).wait_recv()
            rs2s[c, row] = (rs[c, row * PAIR + b].astype(F32) + rs1[c, row].astype(F32)).astype(BF16)
            cp = remote(rs2s.at[c, row], rs2r.at[c, a], r2s_sem.at[c, k - 1], r2r_sem.at[c, a], "mp", row * PAIR + b)
            cp.start()
            r2_copies.append(cp)
    wide = lat_out[...].astype(F32).reshape(n, 8, hid)
    zero = jnp.zeros_like(wide)
    spread_out[0] = jnp.concatenate([wide, zero], axis=1).reshape(n * 16, hid).T.astype(BF16)
    spread_out[1] = jnp.concatenate([zero, wide], axis=1).reshape(n * 16, hid).T.astype(BF16)

    squares = jnp.zeros((), F32)
    g_copies = []
    for c in range(C):
        remote(rs.at[c, 0], rs1.at[c, a], r1s_sem.at[c, A - 1], r1r_sem.at[c, a], "mp", partner).wait_recv()
        total = rs[c, me].astype(F32) + rs1[c, a].astype(F32)
        for k in range(1, A):
            row = lax.rem(a + A - k, A)
            remote(rs2s.at[c, row], rs2r.at[c, row], r2s_sem.at[c, k - 1], r2r_sem.at[c, row], "mp", partner).wait_recv()
            total = total + rs2r[c, row].astype(F32)
        lo, hi = cols_of(c)
        own = jnp.concatenate([act[:, lo].astype(F32), act[:, hi].astype(F32)], axis=0)
        shift = jnp.concatenate([jnp.broadcast_to(dbias[:, lo], (8, cw)), jnp.broadcast_to(dbias[:, hi], (8, cw))], axis=0)
        error = total + shift - own
        squares = squares + jnp.sum(error * error)
        g_all[c, me] = (2.0 * error / T).astype(BF16)
        g_copies += gather_start(g_all, gs_sem, gr_sem, c)

    loss_s[sec] = jnp.full((8, 128), squares / T + penalty, F32)
    l_copies = []
    for k in range(1, ns):
        peer = lax.rem(sec + k, ns)
        cp = remote(loss_s.at[sec], loss_s.at[sec], ls_sem.at[k - 1], lr_sem.at[sec], "section", peer)
        cp.start()
        l_copies.append(cp)
    for c in range(C - 1):
        g_copies += gather_forward(g_all, gs_sem, gr_sem, c)
    for cp in x_copies + p_copies + r1_copies + r2_copies:
        cp.wait_send()
    for k in range(1, ns):
        src = lax.rem(sec + k, ns)
        remote(loss_s.at[src], loss_s.at[src], ls_sem.at[k - 1], lr_sem.at[src], "section", src).wait_recv()
    total = loss_s[0]
    for s in range(1, ns):
        total = total + loss_s[s]
    loss_m[me] = total
    for k in range(1, n):
        peer = lax.rem(me + k, n)
        cp = remote(loss_m.at[me], loss_m.at[me], ms_sem.at[k - 1], mr_sem.at[me], "mp", peer)
        cp.start()
        l_copies.append(cp)
    g_copies += gather_forward(g_all, gs_sem, gr_sem, C - 1)
    for c in range(C - 1):
        gather_finish(g_all, gs_sem, gr_sem, c)
        sums_out[2 * c], sums_out[2 * c + 1] = column_sums(g_all[c])
        for side in range(2):
            cols = cols_of(c)[side]
            for r in range(0, cw, 512):
                grad_block(
                    first_out.at[2 * c + side, :, r:r + 512], spread_out.at[side],
                    g_all[c, :, :, r:r + 512].reshape(n * 16, 512), coef_out,
                    dec_v.at[:, cols.start + r:cols.start + r + 512],
                )
    for k in range(1, n):
        src = lax.rem(me + k, n)
        remote(loss_m.at[src], loss_m.at[src], ms_sem.at[k - 1], mr_sem.at[src], "mp", src).wait_recv()
    total = loss_m[0]
    for s in range(1, n):
        total = total + loss_m[s]
    loss_out[...] = total
    gather_finish(g_all, gs_sem, gr_sem, C - 1)

    def out_step(i):
        g_out[pl.ds(i * TB, TB)] = g_all[C - 1, pl.ds(i * TB, TB)]

    loop(n // TB, out_step)
    for cp in l_copies + g_copies:
        cp.wait_send()


def column_sums(g):
    sums = jnp.sum(g.astype(F32), axis=0)
    shape = (8, sums.shape[1])
    return tuple(
        jnp.broadcast_to(jnp.sum(sums[r:r + 8], axis=0, keepdims=True), shape) for r in (0, 8)
    )


def grad_block(out, spread, g, coef, w):
    width = out.shape[1]
    for r in range(0, out.shape[0], 128):
        total = jnp.dot(spread[r:r + 128, :], g, preferred_element_type=F32)
        scale = jnp.concatenate([coef[r:r + 128, :]] * (width // 128), axis=1)
        out[r:r + 128, :] = (total + scale * w[r:r + 128, :].astype(F32)).astype(BF16)


def grad_kernel(C, width, loss, g, spread, coef, first, sums, w, loss_out, out, bias_out, rest, all_sums, sem):
    n, cw = g.shape[0], g.shape[2]
    half = w.shape[1] // 2
    copies = []
    for c in range(C - 1):
        for side in range(2):
            i = 2 * c + side
            cols = slice(side * half + c * cw, side * half + (c + 1) * cw)
            cp = pltpu.make_async_copy(first.at[i], out.at[:, cols], sem.at[i])
            cp.start()
            copies.append(cp)
    for i in range(2 * (C - 1)):
        all_sums[i] = sums[i]
    slot = 2 * (C - 1)
    for side in range(2):
        for r in range(0, cw, 512):
            start = side * half + (C - 1) * cw + r
            piece = rest.at[side, :, r:r + 512]
            grad_block(piece, spread.at[side], g[:, :, r:r + 512].reshape(n * 16, 512), coef, w.at[:, start:start + 512])
            cp = pltpu.make_async_copy(piece, out.at[:, start:start + 512], sem.at[slot])
            cp.start()
            copies.append(cp)
            slot += 1
    all_sums[2 * C - 2], all_sums[2 * C - 1] = column_sums(g[...])
    loss_out[...] = loss[:1, :1]
    if width % 128 == 0 and cw % width == 0:
        me = lax.axis_index("mp")
        side, place = me // (n // 2), lax.rem(me, n // 2)
        per = cw // width
        cols = pl.ds(pl.multiple_of(lax.rem(place, per) * width, width), width)
        bias_out[...] = all_sums[2 * (place // per) + side, 0:1, cols]
    else:
        for c in range(C):
            for side in range(2):
                start = side * half + c * cw
                bias_out[:, start:start + cw] = all_sums[2 * c + side, 0:1, :]
    for cp in copies:
        cp.wait()


def local(ns, n, activations, enc_weight, enc_bias, dec_weight, dec_bias):
    act = activations[0]
    enc = enc_weight[0]
    w_dec = dec_weight[:, 0, :]
    rows, d = act.shape
    hid = enc.shape[1]
    T = rows * n
    half = d // 2
    A = n // PAIR
    C, HC = 2, 2
    vmem = pl.BlockSpec(memory_space=pltpu.VMEM)
    hbm = pl.BlockSpec(memory_space=pltpu.HBM)
    dma = pltpu.SemaphoreType.DMA
    cw = half // C
    loss, g, spread, coef, first, sums = pl.pallas_call(
        functools.partial(comm_kernel, n, ns, C, HC),
        out_shape=(
            jax.ShapeDtypeStruct((8, 128), F32),
            jax.ShapeDtypeStruct((n, 16, cw), BF16),
            jax.ShapeDtypeStruct((2, hid, n * 16), BF16),
            jax.ShapeDtypeStruct((hid, 128), F32),
            jax.ShapeDtypeStruct((2 * (C - 1), hid, cw), BF16),
            jax.ShapeDtypeStruct((2 * (C - 1), 8, cw), F32),
        ),
        in_specs=[hbm] * 5,
        out_specs=[vmem] * 6,
        scratch_shapes=[
            pltpu.VMEM((rows, d), BF16),
            pltpu.VMEM((1, hid), F32),
            pltpu.VMEM((1, d), F32),
            pltpu.VMEM((T, hid), BF16),
            pltpu.VMEM((C, n, 16, cw), BF16),
            pltpu.VMEM((C, n, 16, cw), BF16),
            pltpu.VMEM((d, hid), BF16),
            pltpu.VMEM((hid, d), BF16),
            pltpu.VMEM((T, hid), F32),
            pltpu.VMEM((HC, ns, T, hid // HC), BF16),
            pltpu.VMEM((C, n, 16, half // C), BF16),
            pltpu.VMEM((C, A, 16, half // C), BF16),
            pltpu.VMEM((C, A, 16, half // C), BF16),
            pltpu.VMEM((C, A, 16, half // C), BF16),
            pltpu.VMEM((hid, 128), F32),
            pltpu.VMEM((ns, 8, 128), F32),
            pltpu.VMEM((n, 8, 128), F32),
            dma((5,)),
            dma((C, 2 * A)), dma((C, n)),
            dma((C, 2 * A)), dma((C, n)),
            dma((HC, ns)), dma((HC, ns)),
            dma((C, A)), dma((C, A)),
            dma((C, A)), dma((C, A)),
            dma((ns,)), dma((ns,)),
            dma((n,)), dma((n,)),
        ],
        compiler_params=pltpu.CompilerParams(
            collective_id=0, has_side_effects=True, vmem_limit_bytes=(28 + n // 4) * 1024 * 1024
        ),
        name="crosscoder_comm",
    )(*(pltpu.with_memory_space_constraint(v, pltpu.HBM) for v in (act, enc, enc_bias[None, :], w_dec, dec_bias)))

    width = d // n
    own = width % 128 == 0 and cw % width == 0
    loss, grad_dec, bias = pl.pallas_call(
        functools.partial(grad_kernel, C, width),
        out_shape=(
            jax.ShapeDtypeStruct((1, 1), F32),
            jax.ShapeDtypeStruct((hid, d), BF16),
            jax.ShapeDtypeStruct((1, width if own else d), F32),
        ),
        in_specs=[vmem] * 7,
        out_specs=[vmem, hbm, vmem],
        scratch_shapes=[
            pltpu.VMEM((2, hid, cw), BF16),
            pltpu.VMEM((2 * C, 8, cw), F32),
            dma((2 * (C - 1) + 2 * (cw // 512),)),
        ],
        compiler_params=pltpu.CompilerParams(vmem_limit_bytes=18 * 1024 * 1024),
        name="grad_dec",
    )(loss, g, spread, coef, first, sums, w_dec)
    if not own:
        bias = lax.dynamic_slice_in_dim(bias, lax.axis_index("mp") * width, width, 1)
    return loss.reshape(()), grad_dec[:, None, :], bias


def solution(mesh):
    in_specs = (
        P("section", "mp", None),
        P("section", None, "mp"),
        P("mp"),
        P("mp", "section", None),
        P("section", None),
    )
    out_specs = (P(), P("mp", "section", None), P("section", "mp"))
    body = functools.partial(local, mesh.shape["section"], mesh.shape["mp"])
    return jax.shard_map(body, mesh=mesh, in_specs=in_specs, out_specs=out_specs, check_vma=False)
```

time: 48.7 us -> 45.1 us (0.926)
  Pallas kernels: 47.9 us -> 44.3 us
    pallas_call x1, Pallas kernels: 4.75 us -> 2.69 us  [local(): pl.pallas_call(functools.partial(grad_kernel, C, width), out_shape=(jax.S...]
    pallas_call x1, Pallas kernels: 43.1 us -> 41.7 us  [local(): pl.pallas_call(functools.partial(comm_kernel, n, ns, C, HC), out_shape=(j...]
where the time goes in v3:
time: 45.1 us; the launch traced here: 45 us
  Pallas kernels  44.3 us (98%)
  between operations  0.66 us (1%)
    pallas_call x1, Pallas kernels, local(): pl.pallas_call(functools.partial(comm_kernel, n, ns, C, HC), out_shape=(j...  41.7 us
    pallas_call x1, Pallas kernels, local(): pl.pallas_call(functools.partial(grad_kernel, C, width), out_shape=(jax.S...  2.69 us

profile of v3, /device:TPU:0, one launch (start us, length us, event | category | flops | bytes accessed | tf_op | source)
XLA Modules:
  0.0 45.0 jit_solution(3661710772518303319)
XLA Ops:
  0.6 0.0 copy-start
  0.6 41.7 %crosscoder_comm.1 = (f32[8,128]{1,0:T(8,128)S(1)}, bf16[8,16,1024]{2,1,0:T(8,128)(2,1)S(1)}, bf16[2,512,128]{2,1,0:T(8,128)(2,1)S(1)}, f32[512,128]{1,0:T(8,128...) custom-call(bf16[8,4096]{1,0:T(8,128)(2,1)} %bitcast.9, bf16[4096,512]{1,0:T(8,128)(2,1)} %bitcast.8, ...), custom_call_target="tpu_custom_call" | custom-call | tf_op jit(solution)/shard_map/crosscoder_comm/pallas_call | solution.py:351
  42.3 0.0 copy-done
  42.3 2.7 %grad_dec.1 = (f32[1,1]{1,0:T(1,128)}, bf16[512,4096]{1,0:T(8,128)(2,1)}, f32[1,512]{1,0:T(1,128)}) custom-call(f32[8,128]{1,0:T(8,128)S(1)} %get-tuple-element.12.loss, bf16[8,16,1024]{2,1,0:T(8,128)(2,1)S(1)} %get-tuple-element.13.g, bf16[2,512,128]{2,1,0:T(8,128)(2,1)S(1)} %get-tuple-element.14.spread, f32[512,128]{1,0:T(8,128)S(1)} %get-tuple-element.15.coef, ...), custom_call_target="tpu_custom_call" | custom-call | tf_op jit(solution)/shard_map/grad_dec/pallas_call | solution.py:398
Async XLA Ops:
  0.6 41.7 %copy-start = (bf16[512,1,4096]{2,0,1:T(8,128)(2,1)S(1)}, bf16[512,1,4096]{2,0,1:T(8,128)(2,1)}, u32[]{:S(2)}) copy-start(bf16[512,1,4096]{2,0,1:T(8,128)(2,1)} %param.8) | copy-start | bytes 12582916

commit v4 on v3

--- a/solution.py
+++ b/solution.py
@@ -22,7 +22,7 @@
 
 
 def comm_kernel(
-    n, ns, C, HC,
+    n, ns, CX, C, CR, HC,
     act_hbm, enc_hbm, bias_hbm, dec_hbm, dbias_hbm,
     loss_out, g_out, spread_out, coef_out, first_out, sums_out,
     act, bias, dbias, lat_out, x_all, g_all, enc_v, dec_v, acc_v, part, rs, rs1, rs2s, rs2r, norm, loss_s, loss_m,
@@ -59,8 +59,13 @@
     def cols_of(c):
         return slice(c * cw, (c + 1) * cw), slice(half + c * cw, half + (c + 1) * cw)
 
-    for c in range(C):
-        lo, hi = cols_of(c)
+    xw = half // CX
+
+    def cols_x(c):
+        return slice(c * xw, (c + 1) * xw), slice(half + c * xw, half + (c + 1) * xw)
+
+    for c in range(CX):
+        lo, hi = cols_x(c)
         x_all[c, me] = jnp.concatenate([act[:, lo].astype(F32), act[:, hi].astype(F32)], axis=0).astype(BF16)
     pl.semaphore_wait(barrier, n - 1 + ns - 1)
 
@@ -98,7 +103,7 @@
             gather_copy(buf, ssem, rsem, c, slot, 0, partner).wait_recv()
 
     x_copies = []
-    for c in range(C):
+    for c in range(CX):
         x_copies += gather_start(x_all, xs_sem, xr_sem, c)
     dec_copy.wait()
 
@@ -112,14 +117,13 @@
         total = jnp.sum(acc, axis=1, keepdims=True)
         norm[rows, :] = jnp.broadcast_to(jnp.sqrt(total + 1e-06), (32, 128))
 
-    for c in range(C):
-        x_copies += gather_forward(x_all, xs_sem, xr_sem, c)
+    x_copies += gather_forward(x_all, xs_sem, xr_sem, 0)
     for cp in (enc_copy, bias_copy, dbias_copy):
         cp.wait()
 
     def enc_chunk(c, i, cols):
-        lo, hi = cols_of(c)
-        x = x_all[c, pl.ds(i * TB, TB)].reshape(TB * 16, cw)
+        lo, hi = cols_x(c)
+        x = x_all[c, pl.ds(i * TB, TB)].reshape(TB * 16, xw)
         left = jnp.dot(x, enc_v[lo, cols], preferred_element_type=F32)
         right = jnp.dot(x, enc_v[hi, cols], preferred_element_type=F32)
         left = left.reshape(TB, 16, left.shape[1])[:, :8]
@@ -129,7 +133,8 @@
     def rows_of(i):
         return pl.ds(pl.multiple_of(i * TB * 8, TB * 8), TB * 8)
 
-    for c in range(C - 1):
+    for c in range(CX - 1):
+        x_copies += gather_forward(x_all, xs_sem, xr_sem, c + 1)
         gather_finish(x_all, xs_sem, xr_sem, c)
 
         def early(i, c=c):
@@ -137,14 +142,16 @@
             acc_v[rows_of(i), :] = value if c == 0 else acc_v[rows_of(i), :] + value
 
         loop(n // TB, early)
-    gather_finish(x_all, xs_sem, xr_sem, C - 1)
+    gather_finish(x_all, xs_sem, xr_sem, CX - 1)
 
     hw = hid // HC
     p_copies = []
     for h in range(HC):
         def enc_step(i, h=h):
             cols = slice(h * hw, (h + 1) * hw)
-            value = acc_v[rows_of(i), cols] + enc_chunk(C - 1, i, cols)
+            value = enc_chunk(CX - 1, i, cols)
+            if CX > 1:
+                value = acc_v[rows_of(i), cols] + value
             part[h, sec, rows_of(i), :] = value.astype(BF16)
 
         loop(n // TB, enc_step)
@@ -168,6 +175,8 @@
 
         loop(n // TB, lat_step)
 
+    rw = half // CR
+
     def r1_start(c, k):
         row = lax.rem(a + k, A)
         cp = remote(rs.at[c, row * PAIR + ob], rs1.at[c, row], r1s_sem.at[c, k - 1], r1r_sem.at[c, row], "mp", partner)
@@ -175,19 +184,19 @@
         return cp
 
     r1_copies = []
-    for c in range(C):
+    for c in range(CR):
         def dec_step(i, c=c):
             rows = pl.ds(pl.multiple_of(i * TB * 8, TB * 8), TB * 8)
             lat = lat_out[rows, :]
-            lo = jnp.dot(lat, dec_v[:, c * cw:(c + 1) * cw], preferred_element_type=F32)
-            hi = jnp.dot(lat, dec_v[:, half + c * cw:half + (c + 1) * cw], preferred_element_type=F32)
-            both = jnp.concatenate([lo.reshape(TB, 8, cw), hi.reshape(TB, 8, cw)], axis=1)
+            lo = jnp.dot(lat, dec_v[:, c * rw:(c + 1) * rw], preferred_element_type=F32)
+            hi = jnp.dot(lat, dec_v[:, half + c * rw:half + (c + 1) * rw], preferred_element_type=F32)
+            both = jnp.concatenate([lo.reshape(TB, 8, rw), hi.reshape(TB, 8, rw)], axis=1)
             rs[c, pl.ds(i * TB, TB)] = both.astype(BF16)
 
         loop(n // TB, dec_step)
         for k in range(1, A):
             r1_copies.append(r1_start(c, k))
-    for c in range(C):
+    for c in range(CR):
         r1_copies.append(r1_start(c, A))
 
     ones = jnp.ones((T, 128), BF16)
@@ -196,7 +205,7 @@
     penalty = penalty_weight / T * jnp.sum(lat_sum[:, :1] * norm[:, :1])
 
     r2_copies = []
-    for c in range(C):
+    for c in range(CR):
         for k in range(1, A):
             row = lax.rem(a + k, A)
             remote(rs.at[c, 0], rs1.at[c, row], r1s_sem.at[c, k - 1], r1r_sem.at[c, row], "mp", partner).wait_recv()
@@ -211,20 +220,23 @@
 
     squares = jnp.zeros((), F32)
     g_copies = []
-    for c in range(C):
+    per = CR // C
+    for c in range(CR):
         remote(rs.at[c, 0], rs1.at[c, a], r1s_sem.at[c, A - 1], r1r_sem.at[c, a], "mp", partner).wait_recv()
         total = rs[c, me].astype(F32) + rs1[c, a].astype(F32)
         for k in range(1, A):
             row = lax.rem(a + A - k, A)
             remote(rs2s.at[c, row], rs2r.at[c, row], r2s_sem.at[c, k - 1], r2r_sem.at[c, row], "mp", partner).wait_recv()
             total = total + rs2r[c, row].astype(F32)
-        lo, hi = cols_of(c)
+        lo, hi = slice(c * rw, (c + 1) * rw), slice(half + c * rw, half + (c + 1) * rw)
         own = jnp.concatenate([act[:, lo].astype(F32), act[:, hi].astype(F32)], axis=0)
-        shift = jnp.concatenate([jnp.broadcast_to(dbias[:, lo], (8, cw)), jnp.broadcast_to(dbias[:, hi], (8, cw))], axis=0)
+        shift = jnp.concatenate([jnp.broadcast_to(dbias[:, lo], (8, rw)), jnp.broadcast_to(dbias[:, hi], (8, rw))], axis=0)
         error = total + shift - own
         squares = squares + jnp.sum(error * error)
-        g_all[c, me] = (2.0 * error / T).astype(BF16)
-        g_copies += gather_start(g_all, gs_sem, gr_sem, c)
+        place = c % per * rw
+        g_all[c // per, me, :, place:place + rw] = (2.0 * error / T).astype(BF16)
+        if c % per == per - 1:
+            g_copies += gather_start(g_all, gs_sem, gr_sem, c // per)
 
     loss_s[sec] = jnp.full((8, 128), squares / T + penalty, F32)
     l_copies = []
@@ -233,8 +245,7 @@
         cp = remote(loss_s.at[sec], loss_s.at[sec], ls_sem.at[k - 1], lr_sem.at[sec], "section", peer)
         cp.start()
         l_copies.append(cp)
-    for c in range(C - 1):
-        g_copies += gather_forward(g_all, gs_sem, gr_sem, c)
+    g_copies += gather_forward(g_all, gs_sem, gr_sem, 0)
     for cp in x_copies + p_copies + r1_copies + r2_copies:
         cp.wait_send()
     for k in range(1, ns):
@@ -249,8 +260,8 @@
         cp = remote(loss_m.at[me], loss_m.at[me], ms_sem.at[k - 1], mr_sem.at[me], "mp", peer)
         cp.start()
         l_copies.append(cp)
-    g_copies += gather_forward(g_all, gs_sem, gr_sem, C - 1)
     for c in range(C - 1):
+        g_copies += gather_forward(g_all, gs_sem, gr_sem, c + 1)
         gather_finish(g_all, gs_sem, gr_sem, c)
         sums_out[2 * c], sums_out[2 * c + 1] = column_sums(g_all[c])
         for side in range(2):
@@ -343,13 +354,13 @@
     T = rows * n
     half = d // 2
     A = n // PAIR
-    C, HC = 2, 2
+    CX, C, CR, HC = 1, 2, 4, 2
     vmem = pl.BlockSpec(memory_space=pltpu.VMEM)
     hbm = pl.BlockSpec(memory_space=pltpu.HBM)
     dma = pltpu.SemaphoreType.DMA
     cw = half // C
     loss, g, spread, coef, first, sums = pl.pallas_call(
-        functools.partial(comm_kernel, n, ns, C, HC),
+        functools.partial(comm_kernel, n, ns, CX, C, CR, HC),
         out_shape=(
             jax.ShapeDtypeStruct((8, 128), F32),
             jax.ShapeDtypeStruct((n, 16, cw), BF16),
@@ -365,25 +376,25 @@
             pltpu.VMEM((1, hid), F32),
             pltpu.VMEM((1, d), F32),
             pltpu.VMEM((T, hid), BF16),
-            pltpu.VMEM((C, n, 16, cw), BF16),
+            pltpu.VMEM((CX, n, 16, half // CX), BF16),
             pltpu.VMEM((C, n, 16, cw), BF16),
             pltpu.VMEM((d, hid), BF16),
             pltpu.VMEM((hid, d), BF16),
             pltpu.VMEM((T, hid), F32),
             pltpu.VMEM((HC, ns, T, hid // HC), BF16),
-            pltpu.VMEM((C, n, 16, half // C), BF16),
-            pltpu.VMEM((C, A, 16, half // C), BF16),
-            pltpu.VMEM((C, A, 16, half // C), BF16),
-            pltpu.VMEM((C, A, 16, half // C), BF16),
+            pltpu.VMEM((CR, n, 16, half // CR), BF16),
+            pltpu.VMEM((CR, A, 16, half // CR), BF16),
+            pltpu.VMEM((CR, A, 16, half // CR), BF16),
+            pltpu.VMEM((CR, A, 16, half // CR), BF16),
             pltpu.VMEM((hid, 128), F32),
             pltpu.VMEM((ns, 8, 128), F32),
             pltpu.VMEM((n, 8, 128), F32),
             dma((5,)),
-            dma((C, 2 * A)), dma((C, n)),
+            dma((CX, 2 * A)), dma((CX, n)),
             dma((C, 2 * A)), dma((C, n)),
             dma((HC, ns)), dma((HC, ns)),
-            dma((C, A)), dma((C, A)),
-            dma((C, A)), dma((C, A)),
+            dma((CR, A)), dma((CR, A)),
+            dma((CR, A)), dma((CR, A)),
             dma((ns,)), dma((ns,)),
             dma((n,)), dma((n,)),
         ],

time: 45.1 us -> 44.5 us (0.987)
  Pallas kernels: 44.3 us -> 43.7 us
    pallas_call x1, Pallas kernels: 41.7 us -> 41 us  [local(): pl.pallas_call(functools.partial(comm_kernel, n, ns, CX, C, CR, HC), out_...]
where the time goes in v4:
time: 44.5 us; the launch traced here: 44.4 us
  Pallas kernels  43.7 us (98%)
  between operations  0.66 us (1%)
    pallas_call x1, Pallas kernels, local(): pl.pallas_call(functools.partial(comm_kernel, n, ns, CX, C, CR, HC), out_...  41 us
    pallas_call x1, Pallas kernels, local(): pl.pallas_call(functools.partial(grad_kernel, C, width), out_shape=(jax.S...  2.69 us

profile of v4, /device:TPU:0, one launch (start us, length us, event | category | flops | bytes accessed | tf_op | source)
XLA Modules:
  0.0 44.4 jit_solution(9106007595197915360)
XLA Ops:
  0.6 0.0 copy-start
  0.6 41.0 %crosscoder_comm.1 = (f32[8,128]{1,0:T(8,128)S(1)}, bf16[8,16,1024]{2,1,0:T(8,128)(2,1)S(1)}, bf16[2,512,128]{2,1,0:T(8,128)(2,1)S(1)}, f32[512,128]{1,0:T(8,128...) custom-call(bf16[8,4096]{1,0:T(8,128)(2,1)} %bitcast.9, bf16[4096,512]{1,0:T(8,128)(2,1)} %bitcast.8, ...), custom_call_target="tpu_custom_call" | custom-call | tf_op jit(solution)/shard_map/crosscoder_comm/pallas_call | solution.py:362
  41.7 0.0 copy-done
  41.7 2.7 %grad_dec.1 = (f32[1,1]{1,0:T(1,128)}, bf16[512,4096]{1,0:T(8,128)(2,1)}, f32[1,512]{1,0:T(1,128)}) custom-call(f32[8,128]{1,0:T(8,128)S(1)} %get-tuple-element.12.loss, bf16[8,16,1024]{2,1,0:T(8,128)(2,1)S(1)} %get-tuple-element.13.g, bf16[2,512,128]{2,1,0:T(8,128)(2,1)S(1)} %get-tuple-element.14.spread, f32[512,128]{1,0:T(8,128)S(1)} %get-tuple-element.15.coef, ...), custom_call_target="tpu_custom_call" | custom-call | tf_op jit(solution)/shard_map/grad_dec/pallas_call | solution.py:409
Async XLA Ops:
  0.6 41.1 %copy-start = (bf16[512,1,4096]{2,0,1:T(8,128)(2,1)S(1)}, bf16[512,1,4096]{2,0,1:T(8,128)(2,1)}, u32[]{:S(2)}) copy-start(bf16[512,1,4096]{2,0,1:T(8,128)(2,1)} %param.8) | copy-start | bytes 12582916
